TPU v7x, 256 devices: a whole 4x4x8 slice. The times are simulated.
256 devices in a mesh: normal: 64 (over x, z, core), span: 4 (over y).
Axes of the slice: x: 4, y: 4, z: 8, core: 2. Of those that a mesh axis runs over, the one named last changes fastest.
Arguments:
- density: float32 [1024, 32, 128], P('normal', 'span'), may hold values from 0.5 to 2
- velocity: float32 [1024, 3, 32, 128], P('normal', None, 'span'), may hold values from -4 to 4
- pressure: float32 [1024, 32, 128], P('normal', 'span'), may hold values from 0.5 to 2
- face_coef: float32 [1024, 5, 5, 32, 128], P('normal', None, None, 'span'), as said below
Outputs:
- update: float32 [1024, 5, 32, 128], P('normal', None, 'span')
Inputs may be any that keep to these rules, and one draw needn't show every extreme that they name: Every 5x5 block face_coef[j, :, :, k, i] is symmetric positive definite with smallest eigenvalue at least 0.1.
All inputs are finite; a program needn't handle non-finite values.
Results may differ from a plain program's by a relative error of at most 0.0003.
Values sent between devices are 32-bit elements; how exact they have to be, the bound alone decides.
A program may use at most 192 MiB of HBM per device.

v0:
```python
import jax
import jax.numpy as jnp
from jax import lax
from jax.sharding import PartitionSpec as P

DIFFUSION = 1000


gamma_gas = 1.4
time_step = 50.0


def padded_2(block, sides, width, periodic):
    for axis, dim in sides:
        count = lax.axis_size(axis)
        forward = [(i, i + 1) for i in range(count - 1)]
        if periodic:
            forward.append((count - 1, 0))
        backward = [(target, source) for source, target in forward]
        low = lax.ppermute(
            lax.slice_in_dim(block, block.shape[dim] - width, None, axis=dim), axis, forward
        )
        high = lax.ppermute(lax.slice_in_dim(block, 0, width, axis=dim), axis, backward)
        block = jnp.concatenate([low, block, high], axis=dim)
    return block


def from_behind(block, axis, distance):
    devices = range(lax.axis_size(axis))
    route = [(i - distance, i) for i in devices if i - distance in devices]
    return lax.ppermute(block, axis, route)


def carried_in(part, axis, combine, identity, reverse):
    count = lax.axis_size(axis)
    place = lax.axis_index(axis)
    ahead = count - 1 - place if reverse else place
    gathered = jax.tree.map(lambda a: lax.all_gather(a, axis), part)
    state = jax.tree.map(lambda a, e: jnp.zeros_like(a) + jnp.asarray(e, a.dtype), part, identity)

    def one(step, state):
        source = count - 1 - step if reverse else step
        return combine(
            state, jax.tree.map(lambda a: lax.dynamic_index_in_dim(a, source, 0, False), gathered)
        )

    return lax.fori_loop(0, ahead, one, state)


def fluxes(density, velocity, pressure):
    speed_sq = jnp.sum(velocity * velocity, axis=1)
    energy = pressure / (gamma_gas - 1.0) + 0.5 * density * speed_sq
    momentum = density[:, None] * velocity
    result = []
    for direction in range(3):
        along_vel = velocity[:, direction]
        pieces = [density * along_vel]
        for component in range(3):
            moment_flux = momentum[:, component] * along_vel
            if component == direction:
                moment_flux = moment_flux + pressure
            pieces.append(moment_flux)
        pieces.append((energy + pressure) * along_vel)
        result.append(jnp.stack(pieces, axis=1))
    return result


def stencil(plus_one, minus_one, plus_two, minus_two):
    return (8.0 * (plus_one - minus_one) - (plus_two - minus_two)) / 12.0


def padded_difference(padded, dim_index, length):

    def shifted(begin):
        return lax.slice_in_dim(padded, begin, begin + length, axis=dim_index)

    return stencil(shifted(3), shifted(1), shifted(4), shifted(0))


def product(left_block, right_block):
    return jnp.sum(left_block[:, :, None, :] * right_block[None, :, :, :], axis=1)


def apply_block(block, vector):
    return jnp.sum(block * vector[None], axis=1)


def eliminate(matrix, values):
    count = matrix.shape[0]
    matrix_rows = [matrix[i] for i in range(count)]
    value_rows = [values[i] for i in range(count)]
    for pivot_at in range(count):
        inverse = 1.0 / matrix_rows[pivot_at][pivot_at]
        matrix_rows[pivot_at] = matrix_rows[pivot_at] * inverse
        value_rows[pivot_at] = value_rows[pivot_at] * inverse
        for other in range(count):
            if other != pivot_at:
                factor = matrix_rows[other][pivot_at]
                matrix_rows[other] = matrix_rows[other] - factor * matrix_rows[pivot_at]
                value_rows[other] = value_rows[other] - factor * value_rows[pivot_at]
    return jnp.stack(value_rows)


def unit_blocks(line_count):
    return jnp.eye(5, dtype=jnp.float32)[:, :, None] * jnp.ones((1, 1, line_count), jnp.float32)


def line_solve(upper_faces, lower_faces, sources):
    line_count = upper_faces.shape[-1]
    columns_count = sources.shape[2]
    unit_block = jnp.eye(5, dtype=jnp.float32)[:, :, None]
    coeff = jnp.float32(DIFFUSION)

    def forward(state_pair, row_data):
        coupled_prev, partial_prev = state_pair
        upper_face, lower_face, values = row_data
        lower = -coeff * lower_face
        matrix = unit_block + coeff * (lower_face + upper_face) - product(lower, coupled_prev)
        columns = jnp.concatenate(
            [-coeff * upper_face, values - product(lower, partial_prev)], axis=1
        )
        solved = eliminate(matrix, columns)
        updated = (solved[:, :5], solved[:, 5:])
        return (updated, updated)

    initial = (
        jnp.zeros((5, 5, line_count), jnp.float32),
        jnp.zeros((5, columns_count, line_count), jnp.float32),
    )
    _, (coupled, partial_value) = lax.scan(forward, initial, (upper_faces, lower_faces, sources))

    def backward(next_value, row_data):
        coupled_row, partial_row = row_data
        value = partial_row - product(coupled_row, next_value)
        return (value, value)

    _, solved = lax.scan(
        backward,
        jnp.zeros((5, columns_count, line_count), jnp.float32),
        (coupled, partial_value),
        reverse=True,
    )
    return solved


def segment_forms(upper_faces, lower_faces, source):
    rows_local = upper_faces.shape[0]
    coeff = jnp.float32(DIFFUSION)
    empty = jnp.zeros(upper_faces.shape, jnp.float32)
    first_cols = empty.at[0].set(coeff * lower_faces[0])
    last_cols = empty.at[rows_local - 1].set(coeff * upper_faces[rows_local - 1])
    columns = jnp.concatenate([source[:, :, None], first_cols, last_cols], axis=2)
    solved = line_solve(upper_faces, lower_faces, columns)
    return (solved[:, :, 0], solved[:, :, 1:6], solved[:, :, 6:11])


def join_segments(left, right):
    line_count = left[0].shape[-1]
    coupling = unit_blocks(line_count) - product(left[5], right[2])
    columns = jnp.concatenate(
        [(left[1] + apply_block(left[5], right[0]))[:, None], left[4], product(left[5], right[3])],
        axis=1,
    )
    solved = eliminate(coupling, columns)
    middle = solved[:, 0]
    middle_left = solved[:, 1:6]
    middle_right = solved[:, 6:11]
    across = right[0] + apply_block(right[2], middle)
    across_left = product(right[2], middle_left)
    across_right = right[3] + product(right[2], middle_right)
    return (
        left[0] + apply_block(left[3], across),
        right[1] + apply_block(right[4], middle),
        left[2] + product(left[3], across_left),
        product(left[3], across_right),
        product(right[4], middle_left),
        right[5] + product(right[4], middle_right),
    )


def combine_forms(left, right):
    joined = join_segments(left, right)
    picked = tuple(
        (
            jnp.where(left[6] > 0.5, right_part, jnp.where(right[6] > 0.5, left_part, joined_part))
            for left_part, right_part, joined_part in zip(left[:6], right[:6], joined)
        )
    )
    return picked + (left[6] * right[6],)


def combine_reversed(earlier, later):
    return combine_forms(later, earlier)


def empty_form(line_count):
    vector = jnp.zeros((5, line_count), jnp.float32)
    block = jnp.zeros((5, 5, line_count), jnp.float32)
    return (vector, vector, block, block, block, block, jnp.ones((), jnp.float32))


def fill_segment(base_part, near_part, far_part, left_value, right_value):
    return (
        base_part
        + jnp.sum(near_part * left_value[None, None], axis=2)
        + jnp.sum(far_part * right_value[None, None], axis=2)
    )


def shards(density, velocity, pressure, face_coef):
    rows_local, _, cells_span, cells_stream = velocity.shape
    line_count = cells_span * cells_stream
    flux_stream, flux_normal, flux_span = fluxes(density, velocity, pressure)
    normal_padded = padded_2(flux_normal, (("normal", 0),), 2, False)
    span_padded = padded_2(flux_span, (("span", 2),), 2, True)
    stream_padded = jnp.pad(flux_stream, ((0, 0), (0, 0), (0, 0), (2, 2)))
    residual = -(
        padded_difference(stream_padded, 3, cells_stream)
        + padded_difference(normal_padded, 0, rows_local)
        + padded_difference(span_padded, 2, cells_span)
    )
    source = (time_step * residual).reshape(rows_local, 5, line_count)
    upper_faces = face_coef.reshape(rows_local, 5, 5, line_count)
    below_face = from_behind(upper_faces[rows_local - 1], "normal", 1)
    lower_faces = jnp.concatenate([below_face[None], upper_faces[:-1]], axis=0)
    base_part, near_part, far_part = segment_forms(upper_faces, lower_faces, source)
    own = (
        base_part[0],
        base_part[-1],
        near_part[0],
        far_part[0],
        near_part[-1],
        far_part[-1],
        jnp.zeros((), jnp.float32),
    )
    below = carried_in(own, "normal", combine_forms, empty_form(line_count), False)
    above = carried_in(own, "normal", combine_reversed, empty_form(line_count), True)
    unit_block = unit_blocks(line_count)
    top_row = jnp.concatenate(
        [unit_block - product(own[2], below[5]), -product(own[3], above[2])], axis=1
    )
    bottom_row = jnp.concatenate(
        [-product(own[4], below[5]), unit_block - product(own[5], above[2])], axis=1
    )
    matrix = jnp.concatenate([top_row, bottom_row], axis=0)
    top_value = own[0] + apply_block(own[2], below[1]) + apply_block(own[3], above[0])
    bottom_value = own[1] + apply_block(own[4], below[1]) + apply_block(own[5], above[0])
    solved = eliminate(matrix, jnp.concatenate([top_value, bottom_value], axis=0)[:, None])[:, 0]
    left_value = below[1] + apply_block(below[5], solved[:5])
    right_value = above[0] + apply_block(above[2], solved[5:])
    update = fill_segment(base_part, near_part, far_part, left_value, right_value)
    return update.reshape(rows_local, 5, cells_span, cells_stream)


def solution(mesh):
    placed = (
        P("normal", "span", None),
        P("normal", None, "span", None),
        P("normal", "span", None),
        P("normal", None, None, "span", None),
    )
    return jax.shard_map(
        shards,
        mesh=mesh,
        in_specs=placed,
        out_specs=P("normal", None, "span", None),
        check_vma=False,
    )
```

profile of v0, /device:TPU:1, one launch (start us, length us, event | category | flops | bytes accessed | tf_op | source)
XLA Modules:
  0.0 1263.6 jit_solution(16424852580069767205)
XLA Ops:
  12.2 3.6 collective-permute-start.2
  16.4 3.6 collective-permute-start
  20.0 2.7 collective-permute-start.1
  23.4 2.4 collective-permute-start.4
  28.7 2.6 copy.93
  31.3 2.6 slice.1271
  33.9 3.2 fusion.81
  38.3 3.1 pad_maximum_fusion.3
  41.4 2.2 select_maximum_fusion
  43.6 3.0 broadcast.1554.clone
  46.7 89.4 %while.82 = (s32[]{:T(128)}, f32[5,5,1024]{2,1,0:T(8,128)S(1)}, f32[5,11,1024]{2,1,0:T(8,128)S(1)}, f32[16,5,5,1024]{3,2,1,0:T(8,128)}, f32[16,5,11,1024]{3,2,1,...) while((s32[]{:T(128)}, f32[5,5,1024]{2,1,0:T(8,128)S(1)}, ...), condition=%wide.region_4.5_spmd.clone, body=%wide.region_1.4_spmd.clone.sunk | while | flops 1923123 | bytes 6837557 | solution.py:130
  136.1 2.9 broadcast.1554
  139.0 62.3 %while.83 = (s32[]{:T(128)}, f32[5,11,1024]{2,1,0:T(8,128)S(1)}, f32[16,5,11,1024]{3,2,1,0:T(8,128)}, f32[16,5,11,1024]{3,2,1,0:T(8,128)}, f32[16,5,5,1024]{3,2,1,0:T(8,128)}, /*index=5*/s32[]{:T(128)}, s32[]{:T(128)}, s32[]{:T(128)}) while((s32[]{:T(128)}, f32[5,11,1024]{2,1,0:T(8,128)S(1)}, f32[16,5,11,1024]{3,2,1,0:T(8,128)}, ...), condition=%wide.region_7.8_spmd.clone, body=%wide.region_5.7_spmd.clone.sunk | while | flops 675844 | bytes 2764919 | solution.py:137
  147.9 1.8 fusion.246
  155.7 1.8 fusion.246
  171.3 1.8 fusion.246
  179.1 1.8 fusion.246
  201.4 4.9 copy.99
  206.3 2.5 copy-done.1
  210.2 2.3 slice_bitcast_fusion.15
  215.7 125.6 %all-reduce.3 = f32[64]{0:T(128)S(1)} all-reduce(f32[64]{0:T(128)S(1)} %dynamic-update-slice.6), channel_id=1, replica_groups=mesh['normal'=64,'span'=4] {'normal'}, use_global_device_ids=true, to_apply=%add.3 | all-reduce | flops 64 | bytes 512
  341.2 1.9 slice.1272
  343.2 2.6 copy.152
  345.8 3.1 copy.151
  348.9 17.4 %all-gather.19.cloned.1.call-done = f32[64,5,1,1024]{3,2,1,0:T(1,128)} async-done(((f32[1,5,1,1024]{3,2,1,0:T(1,128)}), f32[64,5,1,1024]{3,2,1,0:T(1,128)}) %all-gather.19.cloned.1.call-update) | async-done | bytes 1310736 | tf_op jit(solution)/shard_map/all_gather | solution.py:38
  368.1 84.8 %all-gather.11.cloned.1.call-done = f32[64,5,5,1024]{3,2,1,0:T(8,128)} async-done(((f32[1,5,5,1024]{3,2,1,0:T(8,128)}), f32[64,5,5,1024]{3,2,1,0:T(8,128)}) %all-gather.11.cloned.1.call-update) | async-done | bytes 6553616 | tf_op jit(solution)/shard_map/all_gather | solution.py:38
  452.9 85.7 %all-gather.13.cloned.1.call-done = f32[64,5,5,1024]{3,2,1,0:T(8,128)} async-done(((f32[1,5,5,1024]{3,2,1,0:T(8,128)}), f32[64,5,5,1024]{3,2,1,0:T(8,128)}) %all-gather.13.cloned.1.call-update) | async-done | bytes 6553616 | tf_op jit(solution)/shard_map/all_gather | solution.py:38
  538.6 85.7 %all-gather.15.cloned.1.call-done = f32[64,5,5,1024]{3,2,1,0:T(8,128)} async-done(((f32[1,5,5,1024]{3,2,1,0:T(8,128)}), f32[64,5,5,1024]{3,2,1,0:T(8,128)}) %all-gather.15.cloned.1.call-update) | async-done | bytes 6553616 | tf_op jit(solution)/shard_map/all_gather | solution.py:38
  624.3 85.7 %all-gather.9.cloned.1.call-done = f32[64,5,5,1024]{3,2,1,0:T(8,128)} async-done(((f32[1,5,5,1024]{3,2,1,0:T(8,128)}), f32[64,5,5,1024]{3,2,1,0:T(8,128)}) %all-gather.9.cloned.1.call-update) | async-done | bytes 6553616 | tf_op jit(solution)/shard_map/all_gather | solution.py:38
  710.1 516.8 %while.81 = (s32[]{:T(128)}, f32[5,1024]{1,0:T(8,128)S(1)}, f32[5,5,1024]{2,1,0:T(8,128)S(1)}, f32[5,5,1024]{2,1,0:T(8,128)S(1)}, f32[]{:T(128)}, /*index=5*/s32...) while((s32[]{:T(128)}, f32[5,1024]{1,0:T(8,128)S(1)}, ...), condition=%wide.region_27.28_spmd, body=%wide.region_17.27_spmd.sunk | while | flops 2501690 | bytes 7430625 | solution.py:47
  1227.0 8.0 while.80
  1250.2 5.6 multiply_reduce_fusion.19
  (3965 shorter events, 597.2 us)
Async XLA Ops:
  6.5 16.2 %copy-start = (f32[16,5,5,8,128]{4,3,2,1,0:T(8,128)S(1)}, f32[16,5,5,8,128]{4,3,2,1,0:T(8,128)}, u32[]{:S(2)}) copy-start(f32[16,5,5,8,128]{4,3,2,1,0:T(8,128)} %param.19) | copy-start | bytes 4915204
  6.5 336.7 %all-gather.17.cloned.1.call-start = ((), (), s32[]{:S(2)}) async-start(), calls=%async_computation.4 | async-start | bytes 1331200 | tf_op jit(solution)/shard_map/all_gather | solution.py:38
  11.3 15.8 %copy-start.3 = (f32[16,5,8,128]{3,2,0,1:T(8,128)}, f32[16,5,8,128]{3,2,0,1:T(8,128)S(1)}, u32[]{:S(2)}) copy-start(f32[16,5,8,128]{3,2,0,1:T(8,128)S(1)} %get-tuple-element.924) | copy-start | bytes 983044
  11.4 15.8 %copy-start.2 = (f32[16,5,8,128]{3,2,0,1:T(8,128)}, f32[16,5,8,128]{3,2,0,1:T(8,128)S(1)}, u32[]{:S(2)}) copy-start(f32[16,5,8,128]{3,2,0,1:T(8,128)S(1)} %get-tuple-element.1025) | copy-start | bytes 983044
  12.2 21.7 %collective-permute-start.2 = (f32[16,5,2,128]{3,2,0,1:T(2,128)}, f32[16,5,2,128]{3,2,0,1:T(2,128)}, u32[]{:S(2)}, u32[]{:S(2)}) collective-permute-start(f32[16,5,2,128]{3,2,0,1:T(2,128)} %get-tuple-element.1020), channel_id=1, source_target_pairs={{1,0},{2,1},{3,2},{0,3},{5,4},{6,5},{7,6},{4,7},{9,8},{10,9},{11,1... | collective-permute-start | bytes 245768 | tf_op jit(solution)/shard_map/ppermute | solution.py:23
  15.8 18.1 %collective-permute-start.3 = (f32[16,5,2,128]{3,2,0,1:T(2,128)}, f32[16,5,2,128]{3,2,0,1:T(2,128)}, u32[]{:S(2)}, u32[]{:S(2)}) collective-permute-start(f32[16,5,2,128]{3,2,0,1:T(2,128)} %get-tuple-element.1021), channel_id=1, source_target_pairs={{0,1},{1,2},{2,3},{3,0},{4,5},{5,6},{6,7},{7,4},{8,9},{9,10},{10,1... | collective-permute-start | bytes 245768 | tf_op jit(solution)/shard_map/ppermute | solution.py:20
  16.4 17.5 %collective-permute-start = (f32[2,5,8,128]{3,2,0,1:T(8,128)}, f32[2,5,8,128]{3,2,0,1:T(8,128)}, u32[]{:S(2)}, u32[]{:S(2)}) collective-permute-start(f32[2,5,8,128]{3,2,0,1:T(8,128)} %get-tuple-element.1022), channel_id=1, source_target_pairs={{4,0},{8,4},{12,8},{16,12},{20,16},{24,20},{28,24},{32,28},{36,32}... | collective-permute-start | bytes 122888 | tf_op jit(solution)/shard_map/ppermute | solution.py:23
  20.0 13.9 %collective-permute-start.1 = (f32[2,5,8,128]{3,2,0,1:T(8,128)}, f32[2,5,8,128]{3,2,0,1:T(8,128)}, u32[]{:S(2)}, u32[]{:S(2)}) collective-permute-start(f32[2,5,8,128]{3,2,0,1:T(8,128)} %get-tuple-element.1023), channel_id=1, source_target_pairs={{0,4},{4,8},{8,12},{12,16},{16,20},{20,24},{24,28},{28,32},{32,36}... | collective-permute-start | bytes 122888 | tf_op jit(solution)/shard_map/ppermute | solution.py:20
  23.4 14.7 %collective-permute-start.4 = (f32[5,5,1024]{2,1,0:T(8,128)}, f32[5,5,1024]{2,1,0:T(8,128)S(1)}, u32[]{:S(2)}, u32[]{:S(2)}) collective-permute-start(f32[5,5,1024]{2,1,0:T(8,128)} %squeeze.340), channel_id=1, source_target_pairs={{0,4},{4,8},{8,12},{12,16},{16,20},{20,24},{24,28},{28,32},{32,36}... | collective-permute-start | bytes 307208 | tf_op jit(solution)/shard_map/ppermute | solution.py:31
  201.4 13.0 %copy-start.23 = (u32[256]{0:T(256)S(1)}, u32[256]{0:T(256)}, u32[]{:S(2)}) copy-start(u32[256]{0:T(256)} %constant.280) | copy-start | bytes 3076
  206.3 2.5 copy-start.1
  209.4 156.9 %all-gather.19.cloned.1.call-start = ((), (), s32[]{:S(2)}) async-start(), calls=%async_computation.5 | async-start | bytes 1331200 | tf_op jit(solution)/shard_map/all_gather | solution.py:38
  210.2 242.7 %all-gather.11.cloned.1.call-start = ((), (), s32[]{:S(2)}) async-start(), calls=%async_computation.1 | async-start | bytes 10649600 | tf_op jit(solution)/shard_map/all_gather | solution.py:38
  212.6 326.0 %all-gather.13.cloned.1.call-start = ((), (), s32[]{:S(2)}) async-start(), calls=%async_computation.2 | async-start | bytes 10649600 | tf_op jit(solution)/shard_map/all_gather | solution.py:38
  213.2 411.2 %all-gather.15.cloned.1.call-start = ((), (), s32[]{:S(2)}) async-start(), calls=%async_computation.3 | async-start | bytes 10649600 | tf_op jit(solution)/shard_map/all_gather | solution.py:38
  213.7 496.3 %all-gather.9.cloned.1.call-start = ((), (), s32[]{:S(2)}) async-start(), calls=%async_computation | async-start | bytes 10649600 | tf_op jit(solution)/shard_map/all_gather | solution.py:38
  1237.2 1.7 copy-start.4
  1237.5 0.6 copy-start.5
  1237.5 1.1 copy-start.6
  1237.8 0.6 copy-start.7
  1237.8 0.8 copy-start.8
  1237.8 1.1 copy-start.9
  1238.2 0.8 copy-start.10
  1238.2 0.8 copy-start.11
  1238.2 0.8 copy-start.12
  1238.7 0.6 copy-start.14
  1238.7 0.7 copy-start.15
  1238.7 0.7 copy-start.16
  1239.0 1.4 copy-start.18
  1239.0 1.4 copy-start.19
  1239.0 1.4 copy-start.20
  1240.4 2.8 copy-start.22
  (3 other events, 1.9 us)
Sparse Core Ops, SparseCore 0:
  209.6 79.3 all-gather.16
  291.7 74.6 all-gather.18
  369.1 83.7 all-gather.10
  455.5 83.0 all-gather.12
  541.2 83.0 all-gather.14
  626.9 83.0 all-gather.8
where the time goes:
time: 1280 us; the launch traced here: 1260 us
  other arithmetic  407 us (32%)
  waiting for transfers between devices  361 us (28%)
  local copies, waits for them, and re-layouts  237 us (19%)
  blocking collectives  126 us (10%)
  loops' own time  105 us (8%)
  between operations  14.8 us (1%)
    all_gather x6, waiting for transfers between devices, carried_in(): gathered = jax.tree.map(lambda a: lax.all_gather(a, axis), part)  359 us
    reduce_sum x191, other arithmetic, apply_block(): return jnp.sum(block * vector[None], axis=1)  127 us
    unnamed x1, blocking collectives  126 us
    another operation x2, loops' own time, carried_in(): return lax.fori_loop(0, ahead, one, state)  100 us
    select_n x126, other arithmetic, combine_forms(): jnp.where(left[6] > 0.5, right_part, jnp.where(right[6] > 0.5, left_part,...  67.9 us
    add x63, other arithmetic, join_segments(): left[1] + apply_block(left[5], right[0])  58.8 us
    squeeze x62, local copies, waits for them, and re-layouts, one(): lax.dynamic_index_in_dim(a, source, 0, False)  57.9 us
    dynamic_slice x32, local copies, waits for them, and re-layouts, line_solve(): lax.scan(forward, initial, (upper_faces, lower_faces, sources))  46.3 us
  transfers between devices with their start and end apart: 11, of which 5 were waited for; matrix products, arithmetic and copies ran while one was open for 2% of the time, Pallas kernels for 0%

commit v1 on v0

v1 whole, which is shorter than its diff:
```python
import jax
import jax.numpy as jnp
from jax import lax
from jax.experimental import pallas as pl
from jax.experimental.pallas import tpu as pltpu
from jax.sharding import PartitionSpec as P

MESH = pl.DeviceIdType.MESH
DIFFUSION = 1000.0
GAMMA = 1.4
STEP = 50.0
NX, NZ, NC, NS = 4, 8, 2, 4
CELLS = 16
FIVE = range(5)
LL, RR, LR, RL, RH, ELEM = 0, 15, 30, 55, 60, 65
KEPT = 55
ZROWS, BROWS = 72, 16
ORDER = (4, 3, 5, 2, 6, 1, 7)


def tri(i, j):
    low, high = min(i, j), max(i, j)
    return low * 5 - low * (low - 1) // 2 + high - low


def total(terms):
    terms = list(terms)
    while len(terms) > 1:
        terms = [a + b for a, b in zip(terms[::2], terms[1::2])] + terms[len(terms) & ~1 :]
    return terms[0]


def sym_inverse(upper):
    a = list(upper)
    for p in FIVE:
        d = 1.0 / a[tri(p, p)]
        row = [a[tri(p, j)] for j in FIVE]
        scaled = [row[j] * d for j in FIVE]
        for i in FIVE:
            for j in range(i, 5):
                if p not in (i, j):
                    a[tri(i, j)] = a[tri(i, j)] - scaled[i] * row[j]
        for j in FIVE:
            if j != p:
                a[tri(p, j)] = scaled[j]
        a[tri(p, p)] = -d
    return [-v for v in a]


def inverse(rows):
    a = [list(row) for row in rows]
    for p in FIVE:
        d = 1.0 / a[p][p]
        top = [d if j == p else a[p][j] * d for j in FIVE]
        for i in FIVE:
            if i != p:
                f = a[i][p]
                a[i] = [-f * d if j == p else a[i][j] - f * top[j] for j in FIVE]
        a[p] = top
    return a


def combine(left, right, put, keep):
    middle = left(RR, 15) + right(LL, 15)
    inv = sym_inverse([middle[t] for t in range(15)])
    lr1 = [left(LR + 5 * i, 5) for i in FIVE]
    lr2 = [right(LR + 5 * i, 5) for i in FIVE]
    lt1 = [jnp.stack([lr1[i][k] for i in FIVE]) for k in FIVE]
    load = left(RH, 5) + right(RL, 5)
    w1 = [total(inv[tri(i, k)][None] * lt1[k] for k in FIVE) for i in FIVE]
    w2 = [total(inv[tri(i, k)][None] * lr2[k] for k in FIVE) for i in FIVE]
    w = [total(inv[tri(i, k)] * load[k] for k in FIVE) for i in FIVE]
    for i in FIVE:
        keep(5 * i, w1[i])
        keep(25 + 5 * i, w2[i])
        keep(50 + i, w[i][None])
    for i in FIVE:
        t = tri(i, i)
        put(LL + t, left(LL + t, 5 - i) - total(lr1[i][k][None] * w1[k][i:] for k in FIVE))
        put(RR + t, right(RR + t, 5 - i) - total(lr2[k][i][None] * w2[k][i:] for k in FIVE))
        put(LR + 5 * i, -total(lr1[i][k][None] * w2[k] for k in FIVE))
        put(RL + i, left(RL + i, 1) - total(lr1[i][k] * w[k] for k in FIVE)[None])
        put(RH + i, right(RH + i, 1) - total(lr2[k][i] * w[k] for k in FIVE)[None])


def middle_value(kept, low, high):
    rows = []
    for i in FIVE:
        near, far = kept(5 * i, 5), kept(25 + 5 * i, 5)
        rows.append(kept(50 + i, 1)[0] - total(total((near * low, far * high))[k] for k in FIVE))
    return jnp.stack(rows)


def flux(d, v, p, direction):
    along = v[direction]
    energy = p / (GAMMA - 1.0) + 0.5 * d * (v[0] * v[0] + v[1] * v[1] + v[2] * v[2])
    carried = d * along
    pieces = [carried]
    for component in range(3):
        piece = carried * v[component]
        pieces.append(piece + p if component == direction else piece)
    pieces.append((energy + p) * along)
    return pieces


def kernel(
    den, vel, pre, fac, out,
    kf, pd, pv, pp, comp, src, fn, ld, lv, lp, hd, hv, hp, spk, srv, gs, ee, wp, pe,
    zs, zr, ze, wz, xs, xr, xe, wx, bs, br,
    load_sem, near_send, near_recv, z_send, z_recv, x_send, x_recv, b_send, b_recv,
):
    me, row = lax.axis_index("normal"), lax.axis_index("span")
    core = lax.rem(me, NC)
    z = lax.rem(lax.div(me, NC), NZ)
    x = lax.div(me, NC * NZ)
    count = NX * NZ * NC

    def place(x_at, z_at, core_at):
        return ((x_at * NZ + z_at) * NC + core_at, row)

    above = (lax.rem(me + 1, count), row)
    below = (lax.rem(me + count - 1, count), row)
    ahead = (me, lax.rem(row + 1, NS))
    behind = (me, lax.rem(row + NS - 1, NS))
    partner = place(x, z, 1 - core)

    barrier = pltpu.get_barrier_semaphore()
    met = [above, below, ahead, behind, partner]
    met += [place(x, lax.rem(z + o, NZ), c) for o in range(1, NZ) for c in range(NC)]
    met += [place(lax.rem(x + o, NX), z, core) for o in range(1, NX)]
    loads = [
        pltpu.make_async_copy(fac, kf, load_sem.at[0]),
        pltpu.make_async_copy(den, pd, load_sem.at[1]),
        pltpu.make_async_copy(vel, pv, load_sem.at[2]),
        pltpu.make_async_copy(pre, pp, load_sem.at[3]),
    ]
    for copy in loads[1:] + loads[:1]:
        copy.start()
    for device in met:
        pl.semaphore_signal(barrier, inc=1, device_id=device, device_id_type=MESH)
    for copy in loads[1:]:
        copy.wait()

    def send(source, target, number, device):
        return pltpu.make_async_remote_copy(
            src_ref=source, dst_ref=target, send_sem=near_send.at[number],
            recv_sem=near_recv.at[number], device_id=device, device_id_type=MESH,
        )

    tile_row = lax.broadcasted_iota(jnp.int32, (8, 128), 0)
    lane = lax.broadcasted_iota(jnp.int32, (8, 128), 1)
    for number in range(5):
        for g in range(4):
            cells = [
                pd[4 * g + i] if number == 0 else pp[4 * g + i] if number == 4 else pv[4 * g + i, number - 1]
                for i in range(4)
            ]
            first, last = cells[0], cells[3]
            for i in (1, 2, 3):
                first = jnp.where(tile_row >= 2 * i, pltpu.roll(cells[i], 2 * i, 0), first)
            for i in (2, 1, 0):
                last = jnp.where(tile_row < 2 * i + 2, pltpu.roll(cells[i], 2 * i + 2, 0), last)
            spk[0, number, g] = first
            spk[1, number, g] = last
    pl.semaphore_wait(barrier, len(met))
    near = [
        send(spk.at[0], srv.at[1], 0, behind),
        send(spk.at[1], srv.at[0], 1, ahead),
        send(den.at[pl.ds(CELLS - 2, 2)], ld, 2, above),
        send(vel.at[pl.ds(CELLS - 2, 2)], lv, 3, above),
        send(pre.at[pl.ds(CELLS - 2, 2)], lp, 4, above),
        send(den.at[pl.ds(0, 2)], hd, 5, below),
        send(vel.at[pl.ds(0, 2)], hv, 6, below),
        send(pre.at[pl.ds(0, 2)], hp, 7, below),
    ]
    for copy in near:
        copy.start()
    loads[0].wait()

    def invert(g, carry):
        cells = pl.ds(4 * g, 4)
        inv = sym_inverse([kf[cells, i, j] for i in FIVE for j in range(i, 5)])
        inv = [v * (1.0 / DIFFUSION) for v in inv]
        for i in FIVE:
            for j in FIVE:
                comp[cells, i, j] = inv[tri(i, j)]
        return carry

    lax.fori_loop(0, CELLS // 4, invert, 0)

    zero = jnp.zeros((8, 128), jnp.float32)
    one = jnp.ones((8, 128), jnp.float32)
    unit = [jnp.stack([one if i == j else zero for j in FIVE]) for i in FIVE]
    empty = [jnp.stack([zero] * 5)] * 5

    def advance(j, state):
        u, q = state
        q = tuple(q[i] + u[i] for i in FIVE)
        u = tuple(u[i] + total(comp[j, i, k][None] * q[k] for k in FIVE) for i in FIVE)
        return u, q

    b_rows, d_rows = lax.fori_loop(0, CELLS, advance, (tuple(empty), tuple(unit)))
    b_inv = inverse([[b_rows[i][k] for k in FIVE] for i in FIVE])
    for i in FIVE:
        line = jnp.stack(b_inv[i])
        ee[core, LR + 5 * i : LR + 5 * i + 5] = -line
    b_inv_rows = [jnp.stack(b_inv[i]) for i in FIVE]
    for i in FIVE:
        t = RR + tri(i, i)
        ee[core, t : t + 5 - i] = total(d_rows[i][k][None] * b_inv_rows[k][i:] for k in FIVE)
        wp[5 * i : 5 * i + 5] = d_rows[i]
    a_rows, _ = lax.fori_loop(0, CELLS, advance, (tuple(unit), tuple(empty)))
    for i in FIVE:
        t = LL + tri(i, i)
        ee[core, t : t + 5 - i] = total(-ee[core, LR + 5 * i + k][None] * a_rows[k][i:] for k in FIVE)

    for copy in near:
        copy.wait()
    inner_low = jnp.where(me == 0, 0.0, 1.0).astype(jnp.float32)
    inner_high = jnp.where(me == count - 1, 0.0, 1.0).astype(jnp.float32)
    for c in range(2):
        fn[c] = jnp.stack(flux(ld[c], [lv[c, i] for i in range(3)], lp[c], 1)) * inner_low
        fn[CELLS + 2 + c] = jnp.stack(flux(hd[c], [hv[c, i] for i in range(3)], hp[c], 1)) * inner_high

    def normal_flux(j, carry):
        fn[j + 2] = jnp.stack(flux(pd[j], [pv[j, i] for i in range(3)], pp[j], 1))
        return carry

    lax.fori_loop(0, CELLS, normal_flux, 0, unroll=2)
    for side in range(2):
        edge = flux(srv[side, 0], [srv[side, 1 + i] for i in range(3)], srv[side, 4], 2)
        for number in range(5):
            gs[side, number] = edge[number]

    def residual(g, carry):
        low_edge = [gs[0, n, g] for n in FIVE]
        high_edge = [gs[1, n, g] for n in FIVE]
        for i in range(4):
            j = 4 * g + i
            v = [pv[j, a] for a in range(3)]
            along = flux(pd[j], v, pp[j], 0)
            across = flux(pd[j], v, pp[j], 2)
            for n in FIVE:
                f, h = along[n], across[n]
                s1 = jnp.where(lane < 127, pltpu.roll(f, 127, 1), 0.0) - jnp.where(lane > 0, pltpu.roll(f, 1, 1), 0.0)
                s2 = jnp.where(lane < 126, pltpu.roll(f, 126, 1), 0.0) - jnp.where(lane > 1, pltpu.roll(f, 2, 1), 0.0)
                up1 = jnp.where(tile_row < 7, pltpu.roll(h, 7, 0), pltpu.roll(high_edge[n], 7 - 2 * i, 0))
                up2 = jnp.where(tile_row < 6, pltpu.roll(h, 6, 0), pltpu.roll(high_edge[n], (14 - 2 * i) % 8, 0))
                dn1 = jnp.where(tile_row > 0, pltpu.roll(h, 1, 0), pltpu.roll(low_edge[n], 7 - 2 * i, 0))
                dn2 = jnp.where(tile_row > 1, pltpu.roll(h, 2, 0), pltpu.roll(low_edge[n], (8 - 2 * i) % 8, 0))
                t1 = s1 + (up1 - dn1) + (fn[j + 3, n] - fn[j + 1, n])
                t2 = s2 + (up2 - dn2) + (fn[j + 4, n] - fn[j, n])
                src[j, n] = t2 * (STEP / 12.0) - t1 * (8.0 * STEP / 12.0)
        return carry

    lax.fori_loop(0, CELLS // 4, residual, 0)

    def forced(j, state):
        u, q = state
        q = q + (u - src[j])
        u = u + total(comp[j, k] * q[k][None] for k in FIVE)
        return u, q

    a_load, b_load = lax.fori_loop(0, CELLS, forced, (empty[0], empty[0]))
    pull = [-total(ee[core, LR + 5 * i + k] * a_load[k] for k in FIVE) for i in FIVE]
    for i in FIVE:
        ee[core, RL + i] = -pull[i]
        ee[core, RH + i] = total(wp[5 * i + k] * pull[k] for k in FIVE) - b_load[i]

    swap = send(ee.at[core], ee.at[core], 8, partner)
    swap.start()
    swap.wait()

    def write(ref):
        def put(at, value):
            ref[at : at + value.shape[0]] = value

        return put

    def read(ref, *lead):
        return lambda at, size: ref[(*lead, slice(at, at + size))]

    combine(read(ee, 0), read(ee, 1), write(pe), write(wp))

    @pl.when(core == 0)
    def _():
        for s in range(ELEM):
            zs[pl.ds(s, 8, stride=ZROWS), :] = pe[s]
        copies = []
        for o in ORDER:
            there = lax.rem(z + o, NZ)
            copy = pltpu.make_async_remote_copy(
                src_ref=zs.at[pl.ds(pl.multiple_of(there * ZROWS, 8), ZROWS)],
                dst_ref=zr.at[pl.ds(pl.multiple_of(z * ZROWS, 8), ZROWS)],
                send_sem=z_send.at[o], recv_sem=z_recv.at[o],
                device_id=place(x, there, 0), device_id_type=MESH,
            )
            copy.start()
            copies.append(copy)
        mine = pl.ds(pl.multiple_of(z * ZROWS, 8), ZROWS)
        zr[mine] = zs[mine]
        for copy in copies:
            copy.wait()
        for s in range(ELEM):
            ze[s] = zr[pl.ds(s, 8, stride=ZROWS), :]

        def joined(ref, kept, levels):
            def level(step, carry):
                shift = 8 - lax.shift_left(1, step)

                def keep(at, value):
                    kept[step, at : at + value.shape[0]] = value

                combine(
                    read(ref),
                    lambda at, size: pltpu.roll(ref[at : at + size], shift, 1),
                    write(ref),
                    keep,
                )
                return carry

            lax.fori_loop(0, levels, level, 0)

        joined(ze, wz, 3)
        for s in range(ELEM):
            xs[s : s + 1, :] = ze[s, 0:1, :]
        copies = []
        for o in (2, 1, 3):
            copy = pltpu.make_async_remote_copy(
                src_ref=xs,
                dst_ref=xr.at[pl.ds(pl.multiple_of(x * ZROWS, 8), ZROWS)],
                send_sem=x_send.at[o], recv_sem=x_recv.at[o],
                device_id=place(lax.rem(x + o, NX), z, 0), device_id_type=MESH,
            )
            copy.start()
            copies.append(copy)
        xr[pl.ds(pl.multiple_of(x * ZROWS, 8), ZROWS)] = xs[...]
        for o in range(NX, 8):
            xr[pl.ds(o * ZROWS, ZROWS)] = xs[...]
        for copy in copies:
            copy.wait()
        for s in range(ELEM):
            xe[s] = xr[pl.ds(s, 8, stride=ZROWS), :]
        joined(xe, wx, 2)

        inv = sym_inverse([xe[LL + t] for t in range(15)])
        low = jnp.stack([total(inv[tri(i, k)] * xe[RL + k] for k in FIVE) for i in FIVE])
        high = jnp.zeros_like(low)

        def spread(kept, levels, low, high):
            def level(step, ends):
                low, high = ends
                at = levels - 1 - step
                gap = lax.shift_left(1, at)
                mid = middle_value(lambda a, size: kept[at, a : a + size], low, high)
                inside = (lax.bitwise_and(tile_row, gap) != 0)[None]
                return (
                    jnp.where(inside, pltpu.roll(mid, gap, 1), low),
                    jnp.where(inside, pltpu.roll(high, gap, 1), mid),
                )

            return lax.fori_loop(0, levels, level, (low, high))

        low, high = spread(wx, 2, low, high)
        low = pltpu.roll(low, 8 - x, 1)
        high = pltpu.roll(high, 8 - x, 1)
        low, high = spread(wz, 3, low, high)
        for i in FIVE:
            bs[pl.ds(i, 8, stride=BROWS), :] = low[i]
            bs[pl.ds(5 + i, 8, stride=BROWS), :] = high[i]
        mine = pl.ds(pl.multiple_of(z * BROWS, 8), BROWS)
        copies = []
        for o in ORDER + (0,):
            for c in range(NC):
                if o == 0 and c == 0:
                    continue
                there = lax.rem(z + o, NZ)
                copy = pltpu.make_async_remote_copy(
                    src_ref=bs.at[pl.ds(pl.multiple_of(there * BROWS, 8), BROWS)],
                    dst_ref=br.at[mine],
                    send_sem=b_send.at[o, c], recv_sem=b_recv.at[o],
                    device_id=place(x, there, c), device_id_type=MESH,
                )
                copy.start()
                copies.append(copy)
        br[mine] = bs[mine]
        for copy in copies:
            copy.wait_send()

    def arrival(o):
        there = lax.rem(z + o, NZ)
        return pltpu.make_async_remote_copy(
            src_ref=bs.at[pl.ds(0, BROWS)],
            dst_ref=br.at[pl.ds(pl.multiple_of(lax.rem(z + NZ - o, NZ) * BROWS, 8), BROWS)],
            send_sem=b_send.at[o, 0], recv_sem=b_recv.at[o],
            device_id=place(x, there, 1 - core), device_id_type=MESH,
        )

    for o in range(1, NZ):
        arrival(o).wait_recv()

    @pl.when(core == 1)
    def _():
        arrival(0).wait_recv()

    low = jnp.stack([br[pl.ds(i, 8, stride=BROWS), :] for i in FIVE])
    high = jnp.stack([br[pl.ds(5 + i, 8, stride=BROWS), :] for i in FIVE])
    mid = middle_value(read(wp), low, high)
    low, high = jnp.where(core == 0, low, mid), jnp.where(core == 0, mid, high)

    start = []
    for i in FIVE:
        own = total(ee[core, LL + tri(i, k)] * low[k] for k in FIVE)
        other = total(ee[core, LR + 5 * i + k] * high[k] for k in FIVE)
        start.append(ee[core, RL + i] - (own + other))

    def sweep(j, state):
        u, q = state
        out[j] = u
        q = q + (u - src[j])
        u = u + total(comp[j, k] * q[k][None] for k in FIVE)
        return u, q

    lax.fori_loop(0, CELLS, sweep, (low, jnp.stack(start)))


def shards(density, velocity, pressure, face_coef):
    f32 = jnp.float32
    shapes = [
        (CELLS, 5, 5, 8, 128), (CELLS, 8, 128), (CELLS, 3, 8, 128), (CELLS, 8, 128),
        (CELLS, 5, 5, 8, 128), (CELLS, 5, 8, 128), (CELLS + 4, 5, 8, 128),
        (2, 8, 128), (2, 3, 8, 128), (2, 8, 128), (2, 8, 128), (2, 3, 8, 128), (2, 8, 128),
        (2, 5, 4, 8, 128), (2, 5, 4, 8, 128), (2, 5, 4, 8, 128),
        (2, ELEM, 8, 128), (KEPT, 8, 128), (ELEM, 8, 128),
        (8 * ZROWS, 128), (8 * ZROWS, 128), (ELEM, 8, 128), (3, KEPT, 8, 128),
        (ZROWS, 128), (8 * ZROWS, 128), (ELEM, 8, 128), (2, KEPT, 8, 128),
        (8 * BROWS, 128), (8 * BROWS, 128),
    ]
    sems = [(4,), (9,), (9,), (8,), (8,), (4,), (4,), (8, 2), (8,)]
    return pl.pallas_call(
        kernel,
        out_shape=jax.ShapeDtypeStruct((CELLS, 5, 8, 128), f32),
        in_specs=[pl.BlockSpec(memory_space=pl.ANY)] * 4,
        out_specs=pl.BlockSpec(memory_space=pltpu.VMEM),
        scratch_shapes=[pltpu.VMEM(shape, f32) for shape in shapes]
        + [pltpu.SemaphoreType.DMA(shape) for shape in sems],
        compiler_params=pltpu.CompilerParams(collective_id=0, has_side_effects=True),
    )(density, velocity, pressure, face_coef)


def solution(mesh):
    return jax.shard_map(
        shards,
        mesh=mesh,
        in_specs=(
            P("normal", "span", None),
            P("normal", None, "span", None),
            P("normal", "span", None),
            P("normal", None, None, "span", None),
        ),
        out_specs=P("normal", None, "span", None),
        check_vma=False,
    )
```

time: 1280 us -> 37.4 us (0.03); the launches traced: 1260 us -> 37.3 us
  other arithmetic: 407 us -> 0 us
  waiting for transfers between devices: 361 us -> 0 us
  local copies, waits for them, and re-layouts: 237 us -> 1.72 us
  blocking collectives: 126 us -> 0 us
  loops' own time: 105 us -> 0 us
  Pallas kernels: 0 us -> 35.6 us
  between operations: 14.8 us -> 0.01 us
    all_gather x6 -> x0, waiting for transfers between devices: 359 us -> none  [carried_in(): gathered = jax.tree.map(lambda a: lax.all_gather(a, axis), part)]
    reduce_sum x430 -> x0, other arithmetic: 172 us -> none  [the longest x191 127 us: apply_block(): return jnp.sum(block * vector[None], axis=1)]
    unnamed x1 -> x0, blocking collectives: 126 us -> none
    another operation x4 -> x0, loops' own time: 105 us -> none  [the longest x2 100 us: carried_in(): return lax.fori_loop(0, ahead, one, state)]
    dynamic_slice x95 -> x0, local copies, waits for them, and re-layouts: 83.9 us -> none  [the longest x32 46.3 us: line_solve(): lax.scan(forward, initial, (upper_faces, lower_faces, sources))]
    select_n x126 -> x0, other arithmetic: 67.9 us -> none  [combine_forms(): jnp.where(left[6] > 0.5, right_part, jnp.where(right[6] > 0.5, left_part,...]
    add x207 -> x0, other arithmetic: 61.5 us -> none  [the longest x63 58.8 us: join_segments(): left[1] + apply_block(left[5], right[0])]
    squeeze x64 -> x0, local copies, waits for them, and re-layouts: 60.9 us -> none  [the longest x62 57.9 us: one(): lax.dynamic_index_in_dim(a, source, 0, False)]
  transfers between devices with their start and end apart: 11 -> 0, of which waited for: 5 -> 0; matrix products, arithmetic and copies ran while one was open for 2% -> 0% of each run, Pallas kernels for 0% -> 0%
where the time goes in v1:
time: 37.4 us; the launch traced here: 37.3 us
  Pallas kernels  35.6 us (95%)
  local copies, waits for them, and re-layouts  1.72 us (5%)
    pallas_call x1, Pallas kernels, shards(): pl.pallas_call(kernel, out_shape=jax.ShapeDtypeStruct((CELLS, 5, 8, 128),...  35.6 us
    unnamed x1, local copies, waits for them, and re-layouts  1.72 us

profile of v1, /device:TPU:1, one launch (start us, length us, event | category | flops | bytes accessed | tf_op | source)
XLA Modules:
  0.0 37.3 jit_solution(18296962015533447034)
XLA Ops:
  0.0 35.6 %shard_map.46 = f32[16,5,8,128]{3,2,1,0:T(8,128)} custom-call(f32[16,8,128]{2,1,0:T(8,128)} %den.1, f32[16,3,8,128]{3,2,1,0:T(8,128)} %vel.1, f32[16,8,128]{2,1,0:T(8,128)} %pre.1, f32[16,5,5,8,128]{4,3,2,1,0:T(8,128)} %fac.1), custom_call_target="tpu_custom_call" | custom-call | tf_op jit(solution)/shard_map/pallas_call | solution.py:440
  35.6 1.7 %copy.6 = f32[16,5,8,128]{3,2,1,0:T(8,128)} copy(f32[16,5,8,128]{3,2,1,0:T(8,128)} %shard_map.46) | data formatting | bytes 655360

commit v2 on v1

--- a/solution.py
+++ b/solution.py
@@ -13,8 +13,9 @@
 CELLS = 16
 FIVE = range(5)
 LL, RR, LR, RL, RH, ELEM = 0, 15, 30, 55, 60, 65
-KEPT = 55
-ZROWS, BROWS = 72, 16
+MATS = 55
+INV, MID, KEPT = 50, 65, 70
+AROWS, BROWS = 56, 16
 ORDER = (4, 3, 5, 2, 6, 1, 7)
 
 
@@ -60,34 +61,41 @@
     return a
 
 
-def combine(left, right, put, keep):
+def join_matrices(left, right, put, keep):
     middle = left(RR, 15) + right(LL, 15)
     inv = sym_inverse([middle[t] for t in range(15)])
     lr1 = [left(LR + 5 * i, 5) for i in FIVE]
     lr2 = [right(LR + 5 * i, 5) for i in FIVE]
     lt1 = [jnp.stack([lr1[i][k] for i in FIVE]) for k in FIVE]
-    load = left(RH, 5) + right(RL, 5)
     w1 = [total(inv[tri(i, k)][None] * lt1[k] for k in FIVE) for i in FIVE]
     w2 = [total(inv[tri(i, k)][None] * lr2[k] for k in FIVE) for i in FIVE]
-    w = [total(inv[tri(i, k)] * load[k] for k in FIVE) for i in FIVE]
+    for t in range(15):
+        keep(INV + t, inv[t][None])
     for i in FIVE:
         keep(5 * i, w1[i])
         keep(25 + 5 * i, w2[i])
-        keep(50 + i, w[i][None])
     for i in FIVE:
         t = tri(i, i)
         put(LL + t, left(LL + t, 5 - i) - total(lr1[i][k][None] * w1[k][i:] for k in FIVE))
         put(RR + t, right(RR + t, 5 - i) - total(lr2[k][i][None] * w2[k][i:] for k in FIVE))
         put(LR + 5 * i, -total(lr1[i][k][None] * w2[k] for k in FIVE))
-        put(RL + i, left(RL + i, 1) - total(lr1[i][k] * w[k] for k in FIVE)[None])
-        put(RH + i, right(RH + i, 1) - total(lr2[k][i] * w[k] for k in FIVE)[None])
+
+
+def join_loads(left, right, kept, put, keep):
+    load = left(RH, 5) + right(RL, 5)
+    low = left(RL, 5) - total(kept(5 * k, 5) * load[k][None] for k in FIVE)
+    high = right(RH, 5) - total(kept(25 + 5 * k, 5) * load[k][None] for k in FIVE)
+    for i in FIVE:
+        keep(MID + i, total(kept(INV + tri(i, k), 1) * load[k][None] for k in FIVE))
+    put(RL, low)
+    put(RH, high)
 
 
 def middle_value(kept, low, high):
     rows = []
     for i in FIVE:
         near, far = kept(5 * i, 5), kept(25 + 5 * i, 5)
-        rows.append(kept(50 + i, 1)[0] - total(total((near * low, far * high))[k] for k in FIVE))
+        rows.append(kept(MID + i, 1)[0] - total(total((near * low, far * high))[k] for k in FIVE))
     return jnp.stack(rows)
 
 
@@ -105,9 +113,9 @@
 
 def kernel(
     den, vel, pre, fac, out,
-    kf, pd, pv, pp, comp, src, fn, ld, lv, lp, hd, hv, hp, spk, srv, gs, ee, wp, pe,
-    zs, zr, ze, wz, xs, xr, xe, wx, bs, br,
-    load_sem, near_send, near_recv, z_send, z_recv, x_send, x_recv, b_send, b_recv,
+    kf, pd, pv, pp, comp, src, fn, ld, lv, lp, hd, hv, hp, spk, srv, gs, ee, dm, wp, pe,
+    za, zb, ra, rb, ze, wz, xa, xb, qa, qb, xe, wx, bs, br,
+    load_sem, near_send, near_recv, z_send, z_recv, x_send, x_recv, b_send, b_recv, known,
 ):
     me, row = lax.axis_index("normal"), lax.axis_index("span")
     core = lax.rem(me, NC)
@@ -124,22 +132,32 @@
     behind = (me, lax.rem(row + NS - 1, NS))
     partner = place(x, z, 1 - core)
 
+    beside = [place(x, lax.rem(z + o, NZ), core) for o in (1, NZ - 1)]
+    across_x = [place(lax.rem(x + o, NX), z, core) for o in (1, NX - 1)]
     barrier = pltpu.get_barrier_semaphore()
-    met = [above, below, ahead, behind, partner]
-    met += [place(x, lax.rem(z + o, NZ), c) for o in range(1, NZ) for c in range(NC)]
-    met += [place(lax.rem(x + o, NX), z, core) for o in range(1, NX)]
+    met = [above, below, ahead, behind, partner] + beside + across_x
     loads = [
-        pltpu.make_async_copy(fac, kf, load_sem.at[0]),
-        pltpu.make_async_copy(den, pd, load_sem.at[1]),
-        pltpu.make_async_copy(vel, pv, load_sem.at[2]),
-        pltpu.make_async_copy(pre, pp, load_sem.at[3]),
+        pltpu.make_async_copy(den, pd, load_sem.at[0]),
+        pltpu.make_async_copy(vel, pv, load_sem.at[1]),
+        pltpu.make_async_copy(pre, pp, load_sem.at[2]),
     ]
-    for copy in loads[1:] + loads[:1]:
+    blocks = [
+        pltpu.make_async_copy(fac.at[pl.ds(4 * g, 4)], kf.at[pl.ds(4 * g, 4)], load_sem.at[3 + g])
+        for g in range(CELLS // 4)
+    ]
+    for copy in loads + blocks:
         copy.start()
     for device in met:
         pl.semaphore_signal(barrier, inc=1, device_id=device, device_id_type=MESH)
-    for copy in loads[1:]:
+    for copy in loads:
         copy.wait()
+
+    def tell(stage, devices):
+        for device in devices:
+            pl.semaphore_signal(known.at[stage], inc=1, device_id=device, device_id_type=MESH)
+
+    def hear(stage):
+        pl.semaphore_wait(known.at[stage], 2)
 
     def send(source, target, number, device):
         return pltpu.make_async_remote_copy(
@@ -175,10 +193,12 @@
     ]
     for copy in near:
         copy.start()
-    loads[0].wait()
+    tell(0, beside)
+    tell(3, across_x)
 
     def invert(g, carry):
         cells = pl.ds(4 * g, 4)
+        pltpu.make_async_copy(fac.at[cells], kf.at[cells], load_sem.at[3 + g]).wait()
         inv = sym_inverse([kf[cells, i, j] for i in FIVE for j in range(i, 5)])
         inv = [v * (1.0 / DIFFUSION) for v in inv]
         for i in FIVE:
@@ -187,6 +207,9 @@
         return carry
 
     lax.fori_loop(0, CELLS // 4, invert, 0)
+    hear(0)
+    hear(3)
+    tell(1, beside)
 
     zero = jnp.zeros((8, 128), jnp.float32)
     one = jnp.ones((8, 128), jnp.float32)
@@ -208,11 +231,22 @@
     for i in FIVE:
         t = RR + tri(i, i)
         ee[core, t : t + 5 - i] = total(d_rows[i][k][None] * b_inv_rows[k][i:] for k in FIVE)
-        wp[5 * i : 5 * i + 5] = d_rows[i]
+        dm[5 * i : 5 * i + 5] = d_rows[i]
+    hear(1)
+    tell(2, beside)
     a_rows, _ = lax.fori_loop(0, CELLS, advance, (tuple(unit), tuple(empty)))
     for i in FIVE:
         t = LL + tri(i, i)
         ee[core, t : t + 5 - i] = total(-ee[core, LR + 5 * i + k][None] * a_rows[k][i:] for k in FIVE)
+
+    swap = send(ee.at[core, pl.ds(0, MATS)], ee.at[core, pl.ds(0, MATS)], 8, partner)
+    swap.start()
+
+    def normal_flux(j, carry):
+        fn[j + 2] = jnp.stack(flux(pd[j], [pv[j, i] for i in range(3)], pp[j], 1))
+        return carry
+
+    lax.fori_loop(0, CELLS, normal_flux, 0, unroll=2)
 
     for copy in near:
         copy.wait()
@@ -221,12 +255,6 @@
     for c in range(2):
         fn[c] = jnp.stack(flux(ld[c], [lv[c, i] for i in range(3)], lp[c], 1)) * inner_low
         fn[CELLS + 2 + c] = jnp.stack(flux(hd[c], [hv[c, i] for i in range(3)], hp[c], 1)) * inner_high
-
-    def normal_flux(j, carry):
-        fn[j + 2] = jnp.stack(flux(pd[j], [pv[j, i] for i in range(3)], pp[j], 1))
-        return carry
-
-    lax.fori_loop(0, CELLS, normal_flux, 0, unroll=2)
     for side in range(2):
         edge = flux(srv[side, 0], [srv[side, 1 + i] for i in range(3)], srv[side, 4], 2)
         for number in range(5):
@@ -265,85 +293,112 @@
     pull = [-total(ee[core, LR + 5 * i + k] * a_load[k] for k in FIVE) for i in FIVE]
     for i in FIVE:
         ee[core, RL + i] = -pull[i]
-        ee[core, RH + i] = total(wp[5 * i + k] * pull[k] for k in FIVE) - b_load[i]
-
-    swap = send(ee.at[core], ee.at[core], 8, partner)
-    swap.start()
-    swap.wait()
-
-    def write(ref):
+        ee[core, RH + i] = total(dm[5 * i + k] * pull[k] for k in FIVE) - b_load[i]
+
+    swap_loads = send(ee.at[core, pl.ds(MATS, 10)], ee.at[core, pl.ds(MATS, 10)], 9, partner)
+    swap_loads.start()
+
+    def write(ref, *lead):
         def put(at, value):
-            ref[at : at + value.shape[0]] = value
+            ref[(*lead, slice(at, at + value.shape[0]))] = value
 
         return put
 
     def read(ref, *lead):
         return lambda at, size: ref[(*lead, slice(at, at + size))]
 
-    combine(read(ee, 0), read(ee, 1), write(pe), write(wp))
-
-    @pl.when(core == 0)
-    def _():
-        for s in range(ELEM):
-            zs[pl.ds(s, 8, stride=ZROWS), :] = pe[s]
+    swap.wait()
+    join_matrices(read(ee, 0), read(ee, 1), write(pe), write(wp))
+    hear(2)
+
+    def part(at, rows):
+        return pl.ds(pl.multiple_of(at * rows, 8), rows)
+
+    def to_owners(kind, source, target, rows):
         copies = []
         for o in ORDER:
             there = lax.rem(z + o, NZ)
             copy = pltpu.make_async_remote_copy(
-                src_ref=zs.at[pl.ds(pl.multiple_of(there * ZROWS, 8), ZROWS)],
-                dst_ref=zr.at[pl.ds(pl.multiple_of(z * ZROWS, 8), ZROWS)],
-                send_sem=z_send.at[o], recv_sem=z_recv.at[o],
+                src_ref=source.at[part(there, rows)], dst_ref=target.at[part(z, rows)],
+                send_sem=z_send.at[kind, o], recv_sem=z_recv.at[kind, o],
                 device_id=place(x, there, 0), device_id_type=MESH,
             )
             copy.start()
             copies.append(copy)
-        mine = pl.ds(pl.multiple_of(z * ZROWS, 8), ZROWS)
-        zr[mine] = zs[mine]
-        for copy in copies:
-            copy.wait()
-        for s in range(ELEM):
-            ze[s] = zr[pl.ds(s, 8, stride=ZROWS), :]
-
-        def joined(ref, kept, levels):
-            def level(step, carry):
-                shift = 8 - lax.shift_left(1, step)
-
-                def keep(at, value):
-                    kept[step, at : at + value.shape[0]] = value
-
-                combine(
-                    read(ref),
-                    lambda at, size: pltpu.roll(ref[at : at + size], shift, 1),
-                    write(ref),
-                    keep,
-                )
-                return carry
-
-            lax.fori_loop(0, levels, level, 0)
-
-        joined(ze, wz, 3)
-        for s in range(ELEM):
-            xs[s : s + 1, :] = ze[s, 0:1, :]
+        target[part(z, rows)] = source[part(z, rows)]
+        return copies
+
+    def to_columns(kind, source, target, rows):
         copies = []
         for o in (2, 1, 3):
             copy = pltpu.make_async_remote_copy(
-                src_ref=xs,
-                dst_ref=xr.at[pl.ds(pl.multiple_of(x * ZROWS, 8), ZROWS)],
-                send_sem=x_send.at[o], recv_sem=x_recv.at[o],
+                src_ref=source, dst_ref=target.at[part(x, rows)],
+                send_sem=x_send.at[kind, o], recv_sem=x_recv.at[kind, o],
                 device_id=place(lax.rem(x + o, NX), z, 0), device_id_type=MESH,
             )
             copy.start()
             copies.append(copy)
-        xr[pl.ds(pl.multiple_of(x * ZROWS, 8), ZROWS)] = xs[...]
+        target[part(x, rows)] = source[...]
         for o in range(NX, 8):
-            xr[pl.ds(o * ZROWS, ZROWS)] = xs[...]
-        for copy in copies:
+            target[pl.ds(o * rows, rows)] = source[...]
+        return copies
+
+    def turned(ref, step):
+        shift = 8 - lax.shift_left(1, step)
+        return lambda at, size: pltpu.roll(ref[at : at + size], shift, 1)
+
+    def matrix_levels(ref, kept, levels):
+        def level(step, carry):
+            join_matrices(read(ref), turned(ref, step), write(ref), write(kept, step))
+            return carry
+
+        lax.fori_loop(0, levels, level, 0)
+
+    def load_levels(ref, kept, levels):
+        def level(step, carry):
+            join_loads(read(ref), turned(ref, step), read(kept, step), write(ref), write(kept, step))
+            return carry
+
+        lax.fori_loop(0, levels, level, 0)
+
+    @pl.when(core == 0)
+    def _():
+        for s in range(MATS):
+            za[pl.ds(s, 8, stride=AROWS), :] = pe[s]
+        to_owner = to_owners(0, za, ra, AROWS)
+        swap_loads.wait()
+        join_loads(read(ee, 0), read(ee, 1), read(wp), write(pe), write(wp))
+        for s in range(10):
+            zb[pl.ds(s, 8, stride=BROWS), :] = pe[MATS + s]
+        loads_to_owner = to_owners(1, zb, rb, BROWS)
+        for copy in to_owner:
             copy.wait()
-        for s in range(ELEM):
-            xe[s] = xr[pl.ds(s, 8, stride=ZROWS), :]
-        joined(xe, wx, 2)
-
+        for s in range(MATS):
+            ze[s] = ra[pl.ds(s, 8, stride=AROWS), :]
+        matrix_levels(ze, wz, 3)
+        for s in range(MATS):
+            xa[s : s + 1, :] = ze[s, 0:1, :]
+        to_column = to_columns(0, xa, qa, AROWS)
+        for copy in loads_to_owner:
+            copy.wait()
+        for s in range(10):
+            ze[MATS + s] = rb[pl.ds(s, 8, stride=BROWS), :]
+        load_levels(ze, wz, 3)
+        for s in range(10):
+            xb[s : s + 1, :] = ze[MATS + s, 0:1, :]
+        loads_to_column = to_columns(1, xb, qb, BROWS)
+        for copy in to_column:
+            copy.wait()
+        for s in range(MATS):
+            xe[s] = qa[pl.ds(s, 8, stride=AROWS), :]
+        matrix_levels(xe, wx, 2)
         inv = sym_inverse([xe[LL + t] for t in range(15)])
+        for copy in loads_to_column:
+            copy.wait()
+        for s in range(10):
+            xe[MATS + s] = qb[pl.ds(s, 8, stride=BROWS), :]
+        load_levels(xe, wx, 2)
+
         low = jnp.stack([total(inv[tri(i, k)] * xe[RL + k] for k in FIVE) for i in FIVE])
         high = jnp.zeros_like(low)
 
@@ -368,40 +423,38 @@
         for i in FIVE:
             bs[pl.ds(i, 8, stride=BROWS), :] = low[i]
             bs[pl.ds(5 + i, 8, stride=BROWS), :] = high[i]
-        mine = pl.ds(pl.multiple_of(z * BROWS, 8), BROWS)
-        copies = []
-        for o in ORDER + (0,):
+        def serve(there):
             for c in range(NC):
-                if o == 0 and c == 0:
-                    continue
-                there = lax.rem(z + o, NZ)
-                copy = pltpu.make_async_remote_copy(
-                    src_ref=bs.at[pl.ds(pl.multiple_of(there * BROWS, 8), BROWS)],
-                    dst_ref=br.at[mine],
-                    send_sem=b_send.at[o, c], recv_sem=b_recv.at[o],
+                pltpu.make_async_remote_copy(
+                    src_ref=bs.at[pl.ds(there * BROWS, BROWS)], dst_ref=br.at[part(z, BROWS)],
+                    send_sem=b_send.at[there, c], recv_sem=b_recv.at[z],
                     device_id=place(x, there, c), device_id_type=MESH,
-                )
-                copy.start()
-                copies.append(copy)
-        br[mine] = bs[mine]
-        for copy in copies:
-            copy.wait_send()
-
-    def arrival(o):
-        there = lax.rem(z + o, NZ)
-        return pltpu.make_async_remote_copy(
-            src_ref=bs.at[pl.ds(0, BROWS)],
-            dst_ref=br.at[pl.ds(pl.multiple_of(lax.rem(z + NZ - o, NZ) * BROWS, 8), BROWS)],
-            send_sem=b_send.at[o, 0], recv_sem=b_recv.at[o],
-            device_id=place(x, there, 1 - core), device_id_type=MESH,
+                ).start()
+
+        for there in (0, 1, 2, 3, 7, 4, 6, 5):
+            pl.when(there != z)(lambda there=there: serve(there))
+        at_home = pltpu.make_async_remote_copy(
+            src_ref=bs.at[part(z, BROWS)], dst_ref=br.at[part(z, BROWS)],
+            send_sem=b_send.at[z, 1], recv_sem=b_recv.at[z],
+            device_id=partner, device_id_type=MESH,
         )
-
-    for o in range(1, NZ):
-        arrival(o).wait_recv()
+        at_home.start()
+        br[part(z, BROWS)] = bs[part(z, BROWS)]
 
     @pl.when(core == 1)
     def _():
-        arrival(0).wait_recv()
+        swap_loads.wait()
+        join_loads(read(ee, 0), read(ee, 1), read(wp), write(pe), write(wp))
+
+    def arrival(k):
+        return pltpu.make_async_remote_copy(
+            src_ref=bs.at[pl.ds(k * BROWS, BROWS)], dst_ref=br.at[pl.ds(k * BROWS, BROWS)],
+            send_sem=b_send.at[k, 0], recv_sem=b_recv.at[k],
+            device_id=partner, device_id_type=MESH,
+        )
+
+    for k in range(NZ):
+        pl.when(jnp.logical_or(k != z, core == 1))(lambda k=k: arrival(k).wait_recv())
 
     low = jnp.stack([br[pl.ds(i, 8, stride=BROWS), :] for i in FIVE])
     high = jnp.stack([br[pl.ds(5 + i, 8, stride=BROWS), :] for i in FIVE])
@@ -422,6 +475,19 @@
         return u, q
 
     lax.fori_loop(0, CELLS, sweep, (low, jnp.stack(start)))
+
+    @pl.when(core == 0)
+    def _():
+        def sent(there, c):
+            return pltpu.make_async_remote_copy(
+                src_ref=bs.at[pl.ds(there * BROWS, BROWS)], dst_ref=br.at[pl.ds(there * BROWS, BROWS)],
+                send_sem=b_send.at[there, c], recv_sem=b_recv.at[there],
+                device_id=partner, device_id_type=MESH,
+            )
+
+        for there in range(NZ):
+            pl.when(there != z)(lambda there=there: sent(there, 0).wait_send())
+            sent(there, 1).wait_send()
 
 
 def shards(density, velocity, pressure, face_coef):
@@ -431,19 +497,21 @@
         (CELLS, 5, 5, 8, 128), (CELLS, 5, 8, 128), (CELLS + 4, 5, 8, 128),
         (2, 8, 128), (2, 3, 8, 128), (2, 8, 128), (2, 8, 128), (2, 3, 8, 128), (2, 8, 128),
         (2, 5, 4, 8, 128), (2, 5, 4, 8, 128), (2, 5, 4, 8, 128),
-        (2, ELEM, 8, 128), (KEPT, 8, 128), (ELEM, 8, 128),
-        (8 * ZROWS, 128), (8 * ZROWS, 128), (ELEM, 8, 128), (3, KEPT, 8, 128),
-        (ZROWS, 128), (8 * ZROWS, 128), (ELEM, 8, 128), (2, KEPT, 8, 128),
+        (2, ELEM, 8, 128), (25, 8, 128), (KEPT, 8, 128), (ELEM, 8, 128),
+        (8 * AROWS, 128), (8 * BROWS, 128), (8 * AROWS, 128), (8 * BROWS, 128),
+        (ELEM, 8, 128), (3, KEPT, 8, 128),
+        (AROWS, 128), (BROWS, 128), (8 * AROWS, 128), (8 * BROWS, 128), (ELEM, 8, 128), (2, KEPT, 8, 128),
         (8 * BROWS, 128), (8 * BROWS, 128),
     ]
-    sems = [(4,), (9,), (9,), (8,), (8,), (4,), (4,), (8, 2), (8,)]
+    sems = [(7,), (10,), (10,), (2, 8), (2, 8), (2, 4), (2, 4), (8, 2), (8,)]
     return pl.pallas_call(
         kernel,
-        out_shape=jax.ShapeDtypeStruct((CELLS, 5, 8, 128), f32),
+        out_shape=pltpu.VMEM((CELLS, 5, 8, 128), f32),
         in_specs=[pl.BlockSpec(memory_space=pl.ANY)] * 4,
         out_specs=pl.BlockSpec(memory_space=pltpu.VMEM),
         scratch_shapes=[pltpu.VMEM(shape, f32) for shape in shapes]
-        + [pltpu.SemaphoreType.DMA(shape) for shape in sems],
+        + [pltpu.SemaphoreType.DMA(shape) for shape in sems]
+        + [pltpu.SemaphoreType.REGULAR((4,))],
         compiler_params=pltpu.CompilerParams(collective_id=0, has_side_effects=True),
     )(density, velocity, pressure, face_coef)
 

time: 37.4 us -> 32.2 us (0.86)
  Pallas kernels: 35.6 us -> 31.4 us
  local copies, waits for them, and re-layouts: 1.72 us -> 0.73 us
    pallas_call x1, Pallas kernels: 35.6 us -> 31.4 us  [shards(): pl.pallas_call(kernel, out_shape=pltpu.VMEM((CELLS, 5, 8, 128), f32), in_...]
    unnamed x1, local copies, waits for them, and re-layouts: 1.72 us -> 0.73 us
where the time goes in v2:
time: 32.2 us; the launch traced here: 32.1 us
  Pallas kernels  31.4 us (98%)
  local copies, waits for them, and re-layouts  0.73 us (2%)
    pallas_call x1, Pallas kernels, shards(): pl.pallas_call(kernel, out_shape=pltpu.VMEM((CELLS, 5, 8, 128), f32), in_...  31.4 us
    unnamed x1, local copies, waits for them, and re-layouts  0.73 us

profile of v2, /device:TPU:1, one launch (start us, length us, event | category | flops | bytes accessed | tf_op | source)
XLA Modules:
  0.0 32.1 jit_solution(13091033792480523068)
XLA Ops:
  0.0 31.4 %shard_map.46 = f32[16,5,8,128]{3,2,1,0:T(8,128)S(1)} custom-call(f32[16,8,128]{2,1,0:T(8,128)} %den.1, f32[16,3,8,128]{3,2,1,0:T(8,128)} %vel.1, f32[16,8,128]{2,1,0:T(8,128)} %pre.1, f32[16,5,5,8,128]{4,3,2,1,0:T(8,128)} %fac.1), custom_call_target="tpu_custom_call" | custom-call | tf_op jit(solution)/shard_map/pallas_call | solution.py:507
  31.4 0.7 %copy.6 = f32[16,5,8,128]{3,2,1,0:T(8,128)} copy(f32[16,5,8,128]{3,2,1,0:T(8,128)S(1)} %shard_map.46) | data formatting | bytes 655360

commit v3 on v2

--- a/solution.py
+++ b/solution.py
@@ -11,6 +11,7 @@
 STEP = 50.0
 NX, NZ, NC, NS = 4, 8, 2, 4
 CELLS = 16
+FAR, NEAR = STEP / 12.0, 8.0 * STEP / 12.0
 FIVE = range(5)
 LL, RR, LR, RL, RH, ELEM = 0, 15, 30, 55, 60, 65
 MATS = 55
@@ -133,6 +134,7 @@
     partner = place(x, z, 1 - core)
 
     beside = [place(x, lax.rem(z + o, NZ), core) for o in (1, NZ - 1)]
+    two_off = [place(x, lax.rem(z + o, NZ), core) for o in (2, NZ - 2)]
     across_x = [place(lax.rem(x + o, NX), z, core) for o in (1, NX - 1)]
     barrier = pltpu.get_barrier_semaphore()
     met = [above, below, ahead, behind, partner] + beside + across_x
@@ -149,9 +151,6 @@
         copy.start()
     for device in met:
         pl.semaphore_signal(barrier, inc=1, device_id=device, device_id_type=MESH)
-    for copy in loads:
-        copy.wait()
-
     def tell(stage, devices):
         for device in devices:
             pl.semaphore_signal(known.at[stage], inc=1, device_id=device, device_id_type=MESH)
@@ -164,6 +163,24 @@
             src_ref=source, dst_ref=target, send_sem=near_send.at[number],
             recv_sem=near_recv.at[number], device_id=device, device_id_type=MESH,
         )
+
+    pl.semaphore_wait(barrier, len(met))
+    tell(0, beside)
+    tell(2, across_x)
+    near = [
+        send(spk.at[0], srv.at[1], 0, behind),
+        send(spk.at[1], srv.at[0], 1, ahead),
+        send(den.at[pl.ds(CELLS - 2, 2)], ld, 2, above),
+        send(vel.at[pl.ds(CELLS - 2, 2)], lv, 3, above),
+        send(pre.at[pl.ds(CELLS - 2, 2)], lp, 4, above),
+        send(den.at[pl.ds(0, 2)], hd, 5, below),
+        send(vel.at[pl.ds(0, 2)], hv, 6, below),
+        send(pre.at[pl.ds(0, 2)], hp, 7, below),
+    ]
+    for copy in near[2:]:
+        copy.start()
+    for copy in loads:
+        copy.wait()
 
     tile_row = lax.broadcasted_iota(jnp.int32, (8, 128), 0)
     lane = lax.broadcasted_iota(jnp.int32, (8, 128), 1)
@@ -180,21 +197,8 @@
                 last = jnp.where(tile_row < 2 * i + 2, pltpu.roll(cells[i], 2 * i + 2, 0), last)
             spk[0, number, g] = first
             spk[1, number, g] = last
-    pl.semaphore_wait(barrier, len(met))
-    near = [
-        send(spk.at[0], srv.at[1], 0, behind),
-        send(spk.at[1], srv.at[0], 1, ahead),
-        send(den.at[pl.ds(CELLS - 2, 2)], ld, 2, above),
-        send(vel.at[pl.ds(CELLS - 2, 2)], lv, 3, above),
-        send(pre.at[pl.ds(CELLS - 2, 2)], lp, 4, above),
-        send(den.at[pl.ds(0, 2)], hd, 5, below),
-        send(vel.at[pl.ds(0, 2)], hv, 6, below),
-        send(pre.at[pl.ds(0, 2)], hp, 7, below),
-    ]
-    for copy in near:
+    for copy in near[:2]:
         copy.start()
-    tell(0, beside)
-    tell(3, across_x)
 
     def invert(g, carry):
         cells = pl.ds(4 * g, 4)
@@ -208,8 +212,7 @@
 
     lax.fori_loop(0, CELLS // 4, invert, 0)
     hear(0)
-    hear(3)
-    tell(1, beside)
+    tell(1, two_off)
 
     zero = jnp.zeros((8, 128), jnp.float32)
     one = jnp.ones((8, 128), jnp.float32)
@@ -232,15 +235,18 @@
         t = RR + tri(i, i)
         ee[core, t : t + 5 - i] = total(d_rows[i][k][None] * b_inv_rows[k][i:] for k in FIVE)
         dm[5 * i : 5 * i + 5] = d_rows[i]
-    hear(1)
-    tell(2, beside)
+    swaps = [
+        send(ee.at[core, pl.ds(RR, 40)], ee.at[core, pl.ds(RR, 40)], 8, partner),
+        send(ee.at[core, pl.ds(LL, 15)], ee.at[core, pl.ds(LL, 15)], 9, partner),
+        send(ee.at[core, pl.ds(MATS, 10)], ee.at[core, pl.ds(MATS, 10)], 10, partner),
+    ]
+    swaps[0].start()
     a_rows, _ = lax.fori_loop(0, CELLS, advance, (tuple(unit), tuple(empty)))
     for i in FIVE:
         t = LL + tri(i, i)
         ee[core, t : t + 5 - i] = total(-ee[core, LR + 5 * i + k][None] * a_rows[k][i:] for k in FIVE)
 
-    swap = send(ee.at[core, pl.ds(0, MATS)], ee.at[core, pl.ds(0, MATS)], 8, partner)
-    swap.start()
+    swaps[1].start()
 
     def normal_flux(j, carry):
         fn[j + 2] = jnp.stack(flux(pd[j], [pv[j, i] for i in range(3)], pp[j], 1))
@@ -248,21 +254,11 @@
 
     lax.fori_loop(0, CELLS, normal_flux, 0, unroll=2)
 
-    for copy in near:
-        copy.wait()
-    inner_low = jnp.where(me == 0, 0.0, 1.0).astype(jnp.float32)
-    inner_high = jnp.where(me == count - 1, 0.0, 1.0).astype(jnp.float32)
-    for c in range(2):
-        fn[c] = jnp.stack(flux(ld[c], [lv[c, i] for i in range(3)], lp[c], 1)) * inner_low
-        fn[CELLS + 2 + c] = jnp.stack(flux(hd[c], [hv[c, i] for i in range(3)], hp[c], 1)) * inner_high
-    for side in range(2):
-        edge = flux(srv[side, 0], [srv[side, 1 + i] for i in range(3)], srv[side, 4], 2)
-        for number in range(5):
-            gs[side, number] = edge[number]
+    nothing = jnp.zeros((5, 8, 128), jnp.float32)
+    for j in (0, 1, CELLS + 2, CELLS + 3):
+        fn[j] = nothing
 
     def residual(g, carry):
-        low_edge = [gs[0, n, g] for n in FIVE]
-        high_edge = [gs[1, n, g] for n in FIVE]
         for i in range(4):
             j = 4 * g + i
             v = [pv[j, a] for a in range(3)]
@@ -272,16 +268,51 @@
                 f, h = along[n], across[n]
                 s1 = jnp.where(lane < 127, pltpu.roll(f, 127, 1), 0.0) - jnp.where(lane > 0, pltpu.roll(f, 1, 1), 0.0)
                 s2 = jnp.where(lane < 126, pltpu.roll(f, 126, 1), 0.0) - jnp.where(lane > 1, pltpu.roll(f, 2, 1), 0.0)
-                up1 = jnp.where(tile_row < 7, pltpu.roll(h, 7, 0), pltpu.roll(high_edge[n], 7 - 2 * i, 0))
-                up2 = jnp.where(tile_row < 6, pltpu.roll(h, 6, 0), pltpu.roll(high_edge[n], (14 - 2 * i) % 8, 0))
-                dn1 = jnp.where(tile_row > 0, pltpu.roll(h, 1, 0), pltpu.roll(low_edge[n], 7 - 2 * i, 0))
-                dn2 = jnp.where(tile_row > 1, pltpu.roll(h, 2, 0), pltpu.roll(low_edge[n], (8 - 2 * i) % 8, 0))
+                up1 = jnp.where(tile_row < 7, pltpu.roll(h, 7, 0), 0.0)
+                up2 = jnp.where(tile_row < 6, pltpu.roll(h, 6, 0), 0.0)
+                dn1 = jnp.where(tile_row > 0, pltpu.roll(h, 1, 0), 0.0)
+                dn2 = jnp.where(tile_row > 1, pltpu.roll(h, 2, 0), 0.0)
                 t1 = s1 + (up1 - dn1) + (fn[j + 3, n] - fn[j + 1, n])
                 t2 = s2 + (up2 - dn2) + (fn[j + 4, n] - fn[j, n])
-                src[j, n] = t2 * (STEP / 12.0) - t1 * (8.0 * STEP / 12.0)
+                src[j, n] = t2 * FAR - t1 * NEAR
         return carry
 
     lax.fori_loop(0, CELLS // 4, residual, 0)
+
+    for copy in near:
+        copy.wait()
+    inner_low = jnp.where(me == 0, 0.0, 1.0).astype(jnp.float32)
+    inner_high = jnp.where(me == count - 1, 0.0, 1.0).astype(jnp.float32)
+    below_flux, above_flux = [], []
+    for c in range(2):
+        below_flux.append(jnp.stack(flux(ld[c], [lv[c, i] for i in range(3)], lp[c], 1)) * inner_low)
+        above_flux.append(jnp.stack(flux(hd[c], [hv[c, i] for i in range(3)], hp[c], 1)) * inner_high)
+    src[0] = src[0] + (below_flux[1] * NEAR - below_flux[0] * FAR)
+    src[1] = src[1] - below_flux[1] * FAR
+    src[CELLS - 2] = src[CELLS - 2] + above_flux[0] * FAR
+    src[CELLS - 1] = src[CELLS - 1] + (above_flux[1] * FAR - above_flux[0] * NEAR)
+    odd = lax.rem(tile_row, 2) == 1
+    for side in range(2):
+        edge = flux(srv[side, 0], [srv[side, 1 + i] for i in range(3)], srv[side, 4], 2)
+        for n in FIVE:
+            for g in range(4):
+                value = edge[n][g]
+                if side == 0:
+                    gs[side, n, g] = jnp.where(odd, 0.0, pltpu.roll(value, 7, 0) * NEAR) - value * FAR
+                else:
+                    gs[side, n, g] = value * FAR - jnp.where(odd, pltpu.roll(value, 1, 0) * NEAR, 0.0)
+
+    def span_edges(g, carry):
+        for n in FIVE:
+            low, high = gs[0, n, g], gs[1, n, g]
+            for i in range(4):
+                first = low if i == 0 else pltpu.roll(low, 8 - 2 * i, 0)
+                last = high if i == 3 else pltpu.roll(high, 6 - 2 * i, 0)
+                reach = jnp.where(tile_row < 2, first, jnp.where(tile_row > 5, last, 0.0))
+                src[4 * g + i, n] = src[4 * g + i, n] + reach
+        return carry
+
+    lax.fori_loop(0, CELLS // 4, span_edges, 0)
 
     def forced(j, state):
         u, q = state
@@ -289,14 +320,13 @@
         u = u + total(comp[j, k] * q[k][None] for k in FIVE)
         return u, q
 
-    a_load, b_load = lax.fori_loop(0, CELLS, forced, (empty[0], empty[0]))
+    a_load, b_load = lax.fori_loop(0, CELLS, forced, (empty[0], empty[0]), unroll=4)
     pull = [-total(ee[core, LR + 5 * i + k] * a_load[k] for k in FIVE) for i in FIVE]
     for i in FIVE:
         ee[core, RL + i] = -pull[i]
         ee[core, RH + i] = total(dm[5 * i + k] * pull[k] for k in FIVE) - b_load[i]
 
-    swap_loads = send(ee.at[core, pl.ds(MATS, 10)], ee.at[core, pl.ds(MATS, 10)], 9, partner)
-    swap_loads.start()
+    swaps[2].start()
 
     def write(ref, *lead):
         def put(at, value):
@@ -307,26 +337,52 @@
     def read(ref, *lead):
         return lambda at, size: ref[(*lead, slice(at, at + size))]
 
-    swap.wait()
+    swaps[0].wait()
+    swaps[1].wait()
     join_matrices(read(ee, 0), read(ee, 1), write(pe), write(wp))
+    hear(1)
     hear(2)
 
     def part(at, rows):
         return pl.ds(pl.multiple_of(at * rows, 8), rows)
 
-    def to_owners(kind, source, target, rows):
-        copies = []
-        for o in ORDER:
-            there = lax.rem(z + o, NZ)
-            copy = pltpu.make_async_remote_copy(
-                src_ref=source.at[part(there, rows)], dst_ref=target.at[part(z, rows)],
-                send_sem=z_send.at[kind, o], recv_sem=z_recv.at[kind, o],
-                device_id=place(x, there, 0), device_id_type=MESH,
-            )
-            copy.start()
-            copies.append(copy)
-        target[part(z, rows)] = source[part(z, rows)]
-        return copies
+    owner = core == lax.rem(z, 2)
+
+    def to_owner(kind, source, target, rows, o):
+        there = lax.rem(z + o, NZ)
+        return pltpu.make_async_remote_copy(
+            src_ref=source.at[part(there, rows)], dst_ref=target.at[part(z, rows)],
+            send_sem=z_send.at[kind, o], recv_sem=z_recv.at[kind, o],
+            device_id=place(x, there, core), device_id_type=MESH,
+        )
+
+    def to_owners(*piece):
+        @pl.when(owner)
+        def _():
+            kind, source, target, rows = piece
+            for o in (4, 6, 2):
+                to_owner(*piece, o).start()
+            target[part(z, rows)] = source[part(z, rows)]
+
+        @pl.when(jnp.logical_not(owner))
+        def _():
+            for o in (3, 5, 1, 7):
+                to_owner(*piece, o).start()
+
+    def at_owner(*piece):
+        for o in (1, 7, 2, 6, 3, 5, 4):
+            to_owner(*piece, o).wait_recv()
+
+    def sent_to_owners(*piece):
+        @pl.when(owner)
+        def _():
+            for o in (4, 6, 2):
+                to_owner(*piece, o).wait_send()
+
+        @pl.when(jnp.logical_not(owner))
+        def _():
+            for o in (3, 5, 1, 7):
+                to_owner(*piece, o).wait_send()
 
     def to_columns(kind, source, target, rows):
         copies = []
@@ -334,7 +390,7 @@
             copy = pltpu.make_async_remote_copy(
                 src_ref=source, dst_ref=target.at[part(x, rows)],
                 send_sem=x_send.at[kind, o], recv_sem=x_recv.at[kind, o],
-                device_id=place(lax.rem(x + o, NX), z, 0), device_id_type=MESH,
+                device_id=place(lax.rem(x + o, NX), z, core), device_id_type=MESH,
             )
             copy.start()
             copies.append(copy)
@@ -344,7 +400,7 @@
         return copies
 
     def turned(ref, step):
-        shift = 8 - lax.shift_left(1, step)
+        shift = 8 - (1 << step)
         return lambda at, size: pltpu.roll(ref[at : at + size], shift, 1)
 
     def matrix_levels(ref, kept, levels):
@@ -352,35 +408,37 @@
             join_matrices(read(ref), turned(ref, step), write(ref), write(kept, step))
             return carry
 
-        lax.fori_loop(0, levels, level, 0)
+        for step in range(levels):
+            level(step, 0)
 
     def load_levels(ref, kept, levels):
         def level(step, carry):
             join_loads(read(ref), turned(ref, step), read(kept, step), write(ref), write(kept, step))
             return carry
 
-        lax.fori_loop(0, levels, level, 0)
-
-    @pl.when(core == 0)
+        for step in range(levels):
+            level(step, 0)
+
+    pieces = [(0, za, ra, AROWS), (1, zb, rb, BROWS)]
+    for s in range(MATS):
+        za[pl.ds(s, 8, stride=AROWS), :] = pe[s]
+    to_owners(*pieces[0])
+    swaps[2].wait()
+    join_loads(read(ee, 0), read(ee, 1), read(wp), write(pe), write(wp))
+    for s in range(10):
+        zb[pl.ds(s, 8, stride=BROWS), :] = pe[MATS + s]
+    to_owners(*pieces[1])
+
+    @pl.when(owner)
     def _():
-        for s in range(MATS):
-            za[pl.ds(s, 8, stride=AROWS), :] = pe[s]
-        to_owner = to_owners(0, za, ra, AROWS)
-        swap_loads.wait()
-        join_loads(read(ee, 0), read(ee, 1), read(wp), write(pe), write(wp))
-        for s in range(10):
-            zb[pl.ds(s, 8, stride=BROWS), :] = pe[MATS + s]
-        loads_to_owner = to_owners(1, zb, rb, BROWS)
-        for copy in to_owner:
-            copy.wait()
+        at_owner(*pieces[0])
         for s in range(MATS):
             ze[s] = ra[pl.ds(s, 8, stride=AROWS), :]
         matrix_levels(ze, wz, 3)
         for s in range(MATS):
             xa[s : s + 1, :] = ze[s, 0:1, :]
         to_column = to_columns(0, xa, qa, AROWS)
-        for copy in loads_to_owner:
-            copy.wait()
+        at_owner(*pieces[1])
         for s in range(10):
             ze[MATS + s] = rb[pl.ds(s, 8, stride=BROWS), :]
         load_levels(ze, wz, 3)
@@ -406,7 +464,7 @@
             def level(step, ends):
                 low, high = ends
                 at = levels - 1 - step
-                gap = lax.shift_left(1, at)
+                gap = 1 << at
                 mid = middle_value(lambda a, size: kept[at, a : a + size], low, high)
                 inside = (lax.bitwise_and(tile_row, gap) != 0)[None]
                 return (
@@ -414,7 +472,9 @@
                     jnp.where(inside, pltpu.roll(high, gap, 1), mid),
                 )
 
-            return lax.fori_loop(0, levels, level, (low, high))
+            for step in range(levels):
+                low, high = level(step, (low, high))
+            return low, high
 
         low, high = spread(wx, 2, low, high)
         low = pltpu.roll(low, 8 - x, 1)
@@ -423,8 +483,14 @@
         for i in FIVE:
             bs[pl.ds(i, 8, stride=BROWS), :] = low[i]
             bs[pl.ds(5 + i, 8, stride=BROWS), :] = high[i]
+        at_home = pltpu.make_async_remote_copy(
+            src_ref=bs.at[part(z, BROWS)], dst_ref=br.at[part(z, BROWS)],
+            send_sem=b_send.at[z, 0], recv_sem=b_recv.at[z],
+            device_id=partner, device_id_type=MESH,
+        )
+        at_home.start()
         def serve(there):
-            for c in range(NC):
+            for c in (1, 0):
                 pltpu.make_async_remote_copy(
                     src_ref=bs.at[pl.ds(there * BROWS, BROWS)], dst_ref=br.at[part(z, BROWS)],
                     send_sem=b_send.at[there, c], recv_sem=b_recv.at[z],
@@ -433,18 +499,7 @@
 
         for there in (0, 1, 2, 3, 7, 4, 6, 5):
             pl.when(there != z)(lambda there=there: serve(there))
-        at_home = pltpu.make_async_remote_copy(
-            src_ref=bs.at[part(z, BROWS)], dst_ref=br.at[part(z, BROWS)],
-            send_sem=b_send.at[z, 1], recv_sem=b_recv.at[z],
-            device_id=partner, device_id_type=MESH,
-        )
-        at_home.start()
         br[part(z, BROWS)] = bs[part(z, BROWS)]
-
-    @pl.when(core == 1)
-    def _():
-        swap_loads.wait()
-        join_loads(read(ee, 0), read(ee, 1), read(wp), write(pe), write(wp))
 
     def arrival(k):
         return pltpu.make_async_remote_copy(
@@ -454,7 +509,7 @@
         )
 
     for k in range(NZ):
-        pl.when(jnp.logical_or(k != z, core == 1))(lambda k=k: arrival(k).wait_recv())
+        pl.when(jnp.logical_or(k != z, jnp.logical_not(owner)))(lambda k=k: arrival(k).wait_recv())
 
     low = jnp.stack([br[pl.ds(i, 8, stride=BROWS), :] for i in FIVE])
     high = jnp.stack([br[pl.ds(5 + i, 8, stride=BROWS), :] for i in FIVE])
@@ -474,9 +529,12 @@
         u = u + total(comp[j, k] * q[k][None] for k in FIVE)
         return u, q
 
-    lax.fori_loop(0, CELLS, sweep, (low, jnp.stack(start)))
-
-    @pl.when(core == 0)
+    lax.fori_loop(0, CELLS, sweep, (low, jnp.stack(start)), unroll=4)
+
+    for piece in pieces:
+        sent_to_owners(*piece)
+
+    @pl.when(owner)
     def _():
         def sent(there, c):
             return pltpu.make_async_remote_copy(
@@ -486,8 +544,8 @@
             )
 
         for there in range(NZ):
-            pl.when(there != z)(lambda there=there: sent(there, 0).wait_send())
-            sent(there, 1).wait_send()
+            sent(there, 0).wait_send()
+            pl.when(there != z)(lambda there=there: sent(there, 1).wait_send())
 
 
 def shards(density, velocity, pressure, face_coef):
@@ -503,7 +561,7 @@
         (AROWS, 128), (BROWS, 128), (8 * AROWS, 128), (8 * BROWS, 128), (ELEM, 8, 128), (2, KEPT, 8, 128),
         (8 * BROWS, 128), (8 * BROWS, 128),
     ]
-    sems = [(7,), (10,), (10,), (2, 8), (2, 8), (2, 4), (2, 4), (8, 2), (8,)]
+    sems = [(7,), (11,), (11,), (2, 8), (2, 8), (2, 4), (2, 4), (8, 2), (8,)]
     return pl.pallas_call(
         kernel,
         out_shape=pltpu.VMEM((CELLS, 5, 8, 128), f32),

time: 32.2 us -> 31.7 us (0.984)
  Pallas kernels: 31.4 us -> 30.8 us
    pallas_call x1, Pallas kernels: 31.4 us -> 30.8 us  [shards(): pl.pallas_call(kernel, out_shape=pltpu.VMEM((CELLS, 5, 8, 128), f32), in_...]
where the time goes in v3:
time: 31.7 us; the launch traced here: 31.6 us
  Pallas kernels  30.8 us (97%)
  local copies, waits for them, and re-layouts  0.73 us (2%)
    pallas_call x1, Pallas kernels, shards(): pl.pallas_call(kernel, out_shape=pltpu.VMEM((CELLS, 5, 8, 128), f32), in_...  30.8 us
    unnamed x1, local copies, waits for them, and re-layouts  0.73 us

profile of v3, /device:TPU:1, one launch (start us, length us, event | category | flops | bytes accessed | tf_op | source)
XLA Modules:
  0.0 31.6 jit_solution(1877604383193506714)
XLA Ops:
  0.0 30.8 %shard_map.46 = f32[16,5,8,128]{3,2,1,0:T(8,128)S(1)} custom-call(f32[16,8,128]{2,1,0:T(8,128)} %den.1, f32[16,3,8,128]{3,2,1,0:T(8,128)} %vel.1, f32[16,8,128]{2,1,0:T(8,128)} %pre.1, f32[16,5,5,8,128]{4,3,2,1,0:T(8,128)} %fac.1), custom_call_target="tpu_custom_call" | custom-call | tf_op jit(solution)/shard_map/pallas_call | solution.py:565
  30.8 0.7 %copy.6 = f32[16,5,8,128]{3,2,1,0:T(8,128)} copy(f32[16,5,8,128]{3,2,1,0:T(8,128)S(1)} %shard_map.46) | data formatting | bytes 655360
